TPU v7x, 32 devices: a whole 2x2x4 slice. The times are simulated.
32 devices in a mesh: dp: 4 (over y, x), tensor: 8 (over z, core).
Axes of the slice: x: 2, y: 2, z: 4, core: 2. Of those that a mesh axis runs over, the one named last changes fastest.
Arguments:
- activations: bfloat16 [1024, 16384], P('dp', 'tensor'), may hold values from -6 to 6
- angles: float32 [14, 8192], P(None, 'tensor'), may hold values from -3.140625 to 3.140625
- clip_bits: int32 [64, 16384], P('dp', 'tensor'), may hold values from 0 to 65535, as said below
- codes: bfloat16 [16384, 10240], P('tensor', 'dp'), may hold values from -127 to 127, as said below
- exponents: int32 [10240], replicated, may hold values from -16 to -13
- cotangent: bfloat16 [1024, 10240], P('dp', 'tensor'), may hold values from -6 to 6
Outputs:
- input_grad: bfloat16 [1024, 16384], P('dp', 'tensor')
- angle_grad: float32 [14, 8192], P(None, 'tensor')
Inputs may be any that keep to these rules, and one draw needn't show every extreme that they name: Bit k (0 to 15) of clip_bits[w, i] is the clip mask of token 16 w + k at feature i; higher bits are zero. `codes`: every entry is a whole number.
All inputs are finite; a program needn't handle non-finite values.
Results may differ from a plain program's by a relative error of at most 0.003.
Values may be sent and summed in bfloat16 or wider, within the bound.
No kernel may reach another device: no remote copies, remote signals or barrier semaphores. Data moves between devices by JAX's collectives and lax.ppermute only.
A program may use at most 128 MiB of HBM per device.

v0:
```python
import jax
import jax.numpy as jnp
from jax import lax
from jax.sharding import PartitionSpec as P


def partner(value, axis, apart):
    mask = 2**apart
    pairs = [(source, source ^ mask) for source in range(lax.axis_size(axis))]
    return lax.ppermute(value, axis, pairs)


def unpack_mask(clip_bits, rows, width):
    shifts = jnp.arange(16, dtype=jnp.int32)
    bits = jnp.bitwise_and(jnp.right_shift(clip_bits[:, None, :], shifts[None, :, None]), 1)
    return bits.reshape(rows, width).astype(jnp.float32)


def section_terms(table, section, first, width):
    half = 1 << section
    index = first + jnp.arange(width, dtype=jnp.int32)
    pair = jnp.right_shift(index, section + 1) * half + jnp.bitwise_and(index, half - 1)
    theta = jnp.take(table[section], pair)
    lower = jnp.bitwise_and(index, half) == 0
    sign = jnp.where(lower, -1.0, 1.0).astype(jnp.float32)
    return (jnp.cos(theta), sign * jnp.sin(theta), sign, pair)


def local_partner(field, section):
    half = 1 << section
    column = jnp.arange(field.shape[1], dtype=jnp.int32)
    lower = jnp.bitwise_and(column, half) == 0
    return jnp.where(lower[None, :], jnp.roll(field, -half, axis=1), jnp.roll(field, half, axis=1))


def scatter_terms(term, pair, half_pairs):
    return jnp.zeros((half_pairs,), jnp.float32).at[pair].add(term)


def body(activations, angles, clip_bits, codes, exponents, cotangent):
    rows, width = activations.shape
    sections = angles.shape[0]
    share = angles.shape[1]
    half_pairs = share * lax.axis_size("tensor")
    local_count = width.bit_length() - 1
    place = lax.axis_index("tensor")
    table = lax.all_gather(angles, "tensor", axis=1, tiled=True)
    scale = jnp.exp2(exponents.astype(jnp.float32))
    full_cot = lax.all_gather(cotangent, "tensor", axis=1, tiled=True)
    weight_piece = (
        lax.all_gather(codes, "dp", axis=1, tiled=True).astype(jnp.float32) * scale[None, :]
    ).astype(jnp.bfloat16)
    projected = lax.dot_general(
        full_cot, weight_piece, (((1,), (1,)), ((), ())), preferred_element_type=jnp.float32
    )
    grad_rot = projected * unpack_mask(clip_bits, rows, width)
    first = place * width
    field = activations.astype(jnp.float32)
    stored = [None] * sections
    for section in range(sections):
        cosine, signed, sign, pair = section_terms(table, section, first, width)
        if section < local_count:
            other = local_partner(field, section)
        else:
            other = partner(field.astype(jnp.bfloat16), "tensor", section - local_count).astype(
                field.dtype
            )
            stored[section] = (field, other)
        field = cosine * field + signed * other
    grad = grad_rot
    terms_list = [None] * sections
    for section in reversed(range(sections)):
        cosine, signed, sign, pair = section_terms(table, section, first, width)
        if section < local_count:
            other = local_partner(field, section)
            grad_other = local_partner(grad, section)
            before = cosine * field - signed * other
        else:
            before, before_other = stored[section]
            other = cosine * before_other - signed * before
            grad_other = partner(grad, "tensor", section - local_count)
        terms_list[section] = scatter_terms(jnp.sum(sign * grad * other, axis=0), pair, half_pairs)
        grad = cosine * grad - signed * grad_other
        field = before
    input_grad = grad.astype(jnp.bfloat16)
    collected = jnp.stack(terms_list)
    partial_total = lax.psum_scatter(collected, "tensor", scatter_dimension=1, tiled=True)
    angle_grad = lax.psum(partial_total, "dp")
    return (input_grad, angle_grad)


def solution(mesh):
    placed = (
        P("dp", "tensor"),
        P(None, "tensor"),
        P("dp", "tensor"),
        P("tensor", "dp"),
        P(),
        P("dp", "tensor"),
    )
    return jax.shard_map(
        body,
        mesh=mesh,
        in_specs=placed,
        out_specs=(P("dp", "tensor"), P(None, "tensor")),
        check_vma=False,
    )
```

profile of v0, /device:TPU:8, one launch (start us, length us, event | category | flops | bytes accessed | tf_op | source)
XLA Modules:
  0.0 970.6 jit_solution(11110099458539859929)
XLA Ops:
  11.8 16.3 %all_gather.9 = f32[14,8192]{1,0:T(8,128)S(1)} all-gather(f32[14,1024]{1,0:T(8,128)S(1)} %copy-done.17), channel_id=1, replica_groups=mesh['dp'=4,'tensor'=8] {'tensor'}, dimensions={1}, use_global_device_ids=true | all-gather | bytes 516096 | tf_op jit(solution)/shard_map/all_gather | solution.py:47
  28.5 11.8 %gather_fusion = f32[2048]{0:T(1024)S(1)} fusion(f32[8192]{0:T(1024)S(1)} %bitcast.61, s32[2048]{0:T(1024)S(1)} %get-tuple-element.217), kind=kCustom, calls=%fused_computation.clone | custom fusion | bytes 24576 | tf_op jit(solution)/shard_map/jit(_take)/gather | solution.py:23
  40.3 11.8 %gather_fusion.1 = f32[2048]{0:T(1024)S(1)} fusion(f32[8192]{0:T(1024)S(1)} %bitcast.60, s32[2048]{0:T(1024)S(1)} %get-tuple-element.230), kind=kCustom, calls=%fused_computation.1.clone | custom fusion | bytes 24576 | tf_op jit(solution)/shard_map/jit(_take)/gather | solution.py:23
  52.1 11.8 %gather_fusion.2 = f32[2048]{0:T(1024)S(1)} fusion(f32[8192]{0:T(1024)S(1)} %bitcast.59, s32[2048]{0:T(1024)S(1)} %get-tuple-element.218), kind=kCustom, calls=%fused_computation.2.clone | custom fusion | bytes 24576 | tf_op jit(solution)/shard_map/jit(_take)/gather | solution.py:23
  63.9 11.8 %gather_fusion.3 = f32[2048]{0:T(1024)S(1)} fusion(f32[8192]{0:T(1024)S(1)} %bitcast.58, s32[2048]{0:T(1024)S(1)} %get-tuple-element.219), kind=kCustom, calls=%fused_computation.3.clone | custom fusion | bytes 24576 | tf_op jit(solution)/shard_map/jit(_take)/gather | solution.py:23
  75.7 11.8 %gather_fusion.4 = f32[2048]{0:T(1024)S(1)} fusion(f32[8192]{0:T(1024)S(1)} %bitcast.57, s32[2048]{0:T(1024)S(1)} %get-tuple-element.220), kind=kCustom, calls=%fused_computation.4.clone | custom fusion | bytes 24576 | tf_op jit(solution)/shard_map/jit(_take)/gather | solution.py:23
  87.5 11.8 %gather_fusion.5 = f32[2048]{0:T(1024)S(1)} fusion(f32[8192]{0:T(1024)S(1)} %bitcast.56, s32[2048]{0:T(1024)S(1)} %get-tuple-element.221), kind=kCustom, calls=%fused_computation.5.clone | custom fusion | bytes 24576 | tf_op jit(solution)/shard_map/jit(_take)/gather | solution.py:23
  99.3 11.8 %gather_fusion.6 = f32[2048]{0:T(1024)S(1)} fusion(f32[8192]{0:T(1024)S(1)} %bitcast.55, s32[2048]{0:T(1024)S(1)} %get-tuple-element.222), kind=kCustom, calls=%fused_computation.6.clone | custom fusion | bytes 24576 | tf_op jit(solution)/shard_map/jit(_take)/gather | solution.py:23
  111.1 11.8 %gather_fusion.7 = f32[2048]{0:T(1024)S(1)} fusion(f32[8192]{0:T(1024)S(1)} %bitcast.54, s32[2048]{0:T(1024)S(1)} %get-tuple-element.223), kind=kCustom, calls=%fused_computation.7.clone | custom fusion | bytes 24576 | tf_op jit(solution)/shard_map/jit(_take)/gather | solution.py:23
  122.9 11.8 %gather_fusion.8 = f32[2048]{0:T(1024)S(1)} fusion(f32[8192]{0:T(1024)S(1)} %bitcast.53, s32[2048]{0:T(1024)S(1)} %get-tuple-element.224), kind=kCustom, calls=%fused_computation.8.clone | custom fusion | bytes 24576 | tf_op jit(solution)/shard_map/jit(_take)/gather | solution.py:23
  134.7 11.8 %gather_fusion.9 = f32[2048]{0:T(1024)S(1)} fusion(f32[8192]{0:T(1024)S(1)} %bitcast.52, s32[2048]{0:T(1024)S(1)} %get-tuple-element.225), kind=kCustom, calls=%fused_computation.9.clone | custom fusion | bytes 24576 | tf_op jit(solution)/shard_map/jit(_take)/gather | solution.py:23
  187.3 249.5 %all-gather.3.cloned.1.call-done = bf16[2048,10240]{1,0:T(8,128)(2,1)} async-done(((bf16[2048,2560]{1,0:T(8,128)(2,1)}), bf16[2048,10240]{1,0:T(8,128)(2,1)}) %all-gather.3.cloned.1.call-update) | async-done | bytes 41943056 | tf_op jit(solution)/shard_map/all_gather | solution.py:51
  436.8 20.6 %fusion.3 = f32[256,2048]{0,1:T(8,128)} fusion(bf16[256,10240]{1,0:T(8,128)(2,1)} %all-gather.5.cloned.1.call-done, bf16[2048,10240]{1,0:T(8,128)(2,1)} %all-gather.3.cloned.1.call-done, f32[10240]{0:T(1024)S(1)} %multiply_exponential_fusion, s32[256,2048]{0,1:T(8,128)S(1)} %copy-done.2, s32[256]{0:T(256)S(1)} %shift_right_arithmetic.224), kind=kOutput, calls=%fused_computation.32 | convolution fusion | flops 10802429952 | bytes 51422208 | tf_op jit(solution)/shard_map/dot_general | solution.py:53
  474.6 11.8 %gather_fusion.13 = f32[2048]{0:T(1024)S(1)} fusion(f32[8192]{0:T(1024)S(1)} %bitcast.49, s32[2048]{0:T(1024)S(1)} %get-tuple-element.229), kind=kCustom, calls=%fused_computation.13.clone | custom fusion | bytes 24576 | tf_op jit(solution)/shard_map/jit(_take)/gather | solution.py:23
  488.5 61.2 %collective-permute-done = f32[256,2048]{0,1:T(8,128)} collective-permute-done((f32[256,2048]{0,1:T(8,128)}, f32[256,2048]{0,1:T(8,128)}, u32[]{:S(2)}, u32[]{:S(2)}) %collective-permute-start) | collective-permute-done | bytes 2097184 | tf_op jit(solution)/shard_map/ppermute | solution.py:10
  571.8 53.3 %collective-permute-done.5 = bf16[256,2048]{0,1:T(8,128)(2,1)S(1)} collective-permute-done((bf16[256,2048]{0,1:T(8,128)(2,1)S(1)}, bf16[256,2048]{0,1:T(8,128)(2,1)S(1)}, u32[]{:S(2)}, u32[]{:S(2)}) %collective-permute-start.5) | collective-permute-done | bytes 1048608 | tf_op jit(solution)/shard_map/ppermute | solution.py:10
  638.3 14.7 %scatter_custom_fusion.13 = f32[8192]{0:T(1024)S(1)} fusion(s32[2048]{0:T(1024)S(1)} %bitcast.90, f32[2048]{0:T(1024)S(1)} %get-tuple-element.7, f32[]{:T(128)} %constant.42.clone.1), kind=kCustom, calls=%fused_computation.177 | custom fusion | flops 2048 | bytes 32772 | tf_op jit(solution)/shard_map/scatter-add | solution.py:37
  653.0 14.7 %scatter_custom_fusion.12 = f32[8192]{0:T(1024)S(1)} fusion(s32[2048]{0:T(1024)S(1)} %bitcast.89, f32[2048]{0:T(1024)S(1)} %get-tuple-element.8, f32[]{:T(128)} %constant.42.clone.1), kind=kCustom, calls=%fused_computation.179 | custom fusion | flops 2048 | bytes 32772 | tf_op jit(solution)/shard_map/scatter-add | solution.py:37
  667.8 14.7 %scatter_custom_fusion.11 = f32[8192]{0:T(1024)S(1)} fusion(s32[2048]{0:T(1024)S(1)} %bitcast.88, f32[2048]{0:T(1024)S(1)} %get-tuple-element.9, f32[]{:T(128)} %constant.42.clone.1), kind=kCustom, calls=%fused_computation.181 | custom fusion | flops 2048 | bytes 32772 | tf_op jit(solution)/shard_map/scatter-add | solution.py:37
  746.0 14.9 %scatter_custom_fusion.10 = f32[8192]{0:T(1024)S(1)} fusion(s32[2048]{0:T(1024)} %bitcast.83, f32[2048]{0:T(1024)S(1)} %get-tuple-element.13, f32[]{:T(128)} %constant.42.clone.1), kind=kCustom, calls=%fused_computation.183 | custom fusion | flops 2048 | bytes 33280 | tf_op jit(solution)/shard_map/scatter-add | solution.py:37
  760.8 14.9 %scatter_custom_fusion.9 = f32[8192]{0:T(1024)S(1)} fusion(s32[2048]{0:T(1024)} %bitcast.86, f32[2048]{0:T(1024)S(1)} %get-tuple-element.15, f32[]{:T(128)} %constant.42.clone.1), kind=kCustom, calls=%fused_computation.185 | custom fusion | flops 2048 | bytes 33280 | tf_op jit(solution)/shard_map/scatter-add | solution.py:37
  775.7 14.9 %scatter_custom_fusion.8 = f32[8192]{0:T(1024)S(1)} fusion(s32[2048]{0:T(1024)} %bitcast.84, f32[2048]{0:T(1024)S(1)} %get-tuple-element.17, f32[]{:T(128)} %constant.42.clone.1), kind=kCustom, calls=%fused_computation.187 | custom fusion | flops 2048 | bytes 33280 | tf_op jit(solution)/shard_map/scatter-add | solution.py:37
  790.5 14.9 %scatter_custom_fusion.7 = f32[8192]{0:T(1024)S(1)} fusion(s32[2048]{0:T(1024)} %bitcast.87, f32[2048]{0:T(1024)S(1)} %get-tuple-element.19, f32[]{:T(128)} %constant.42.clone.1), kind=kCustom, calls=%fused_computation.189 | custom fusion | flops 2048 | bytes 33280 | tf_op jit(solution)/shard_map/scatter-add | solution.py:37
  805.4 15.1 %scatter_custom_fusion.6 = f32[8192]{0:T(1024)S(1)} fusion(s32[2048]{0:T(1024)} %bitcast.85, f32[2048]{0:T(1024)S(1)} %get-tuple-element.21, f32[]{:T(128)} %constant.42.clone.1), kind=kCustom, calls=%fused_computation.191 | custom fusion | flops 2048 | bytes 33280 | tf_op jit(solution)/shard_map/scatter-add | solution.py:37
  820.5 14.9 %scatter_custom_fusion.5 = f32[8192]{0:T(1024)S(1)} fusion(s32[2048]{0:T(1024)} %bitcast.82, f32[2048]{0:T(1024)S(1)} %get-tuple-element.23, f32[]{:T(128)} %constant.42.clone.1), kind=kCustom, calls=%fused_computation.193 | custom fusion | flops 2048 | bytes 33280 | tf_op jit(solution)/shard_map/scatter-add | solution.py:37
  835.4 14.9 %scatter_custom_fusion.4 = f32[8192]{0:T(1024)S(1)} fusion(s32[2048]{0:T(1024)} %bitcast.80, f32[2048]{0:T(1024)S(1)} %get-tuple-element.25, f32[]{:T(128)} %constant.42.clone.1), kind=kCustom, calls=%fused_computation.195 | custom fusion | flops 2048 | bytes 33280 | tf_op jit(solution)/shard_map/scatter-add | solution.py:37
  850.2 14.9 %scatter_custom_fusion.3 = f32[8192]{0:T(1024)S(1)} fusion(s32[2048]{0:T(1024)} %bitcast.81, f32[2048]{0:T(1024)S(1)} %get-tuple-element.27, f32[]{:T(128)} %constant.42.clone.1), kind=kCustom, calls=%fused_computation.197 | custom fusion | flops 2048 | bytes 33280 | tf_op jit(solution)/shard_map/scatter-add | solution.py:37
  865.1 14.9 %scatter_custom_fusion.2 = f32[8192]{0:T(1024)S(1)} fusion(s32[2048]{0:T(1024)} %bitcast.79, f32[2048]{0:T(1024)S(1)} %get-tuple-element.29, f32[]{:T(128)} %constant.42.clone.1), kind=kCustom, calls=%fused_computation.199 | custom fusion | flops 2048 | bytes 33280 | tf_op jit(solution)/shard_map/scatter-add | solution.py:37
  880.0 14.9 %scatter_custom_fusion.1 = f32[8192]{0:T(1024)S(1)} fusion(s32[2048]{0:T(1024)} %bitcast.78, f32[2048]{0:T(1024)S(1)} %get-tuple-element.31, f32[]{:T(128)} %constant.42.clone.1), kind=kCustom, calls=%fused_computation.201 | custom fusion | flops 2048 | bytes 33280 | tf_op jit(solution)/shard_map/scatter-add | solution.py:37
  901.3 14.9 %scatter_custom_fusion = f32[8192]{0:T(1024)S(1)} fusion(s32[2048]{0:T(1024)} %bitcast.77, f32[2048]{0:T(1024)S(1)} %get-tuple-element.33, f32[]{:T(128)} %constant.42.clone.1), kind=kCustom, calls=%fused_computation.203 | custom fusion | flops 2048 | bytes 33280 | tf_op jit(solution)/shard_map/scatter-add | solution.py:37
  924.6 20.9 %reduce-scatter.2.cloned.1.call-done = f32[14,1024]{1,0:T(8,128)} async-done(((f32[14,8192]{1,0:T(8,128)}), f32[14,1024]{1,0:T(8,128)}) %reduce-scatter.2.cloned.1.call-update) | async-done | bytes 57360 | tf_op jit(solution)/shard_map/reduce_scatter | solution.py:87
  945.5 18.1 %psum.7 = f32[14,1024]{1,0:T(8,128)} all-reduce(f32[14,1024]{1,0:T(8,128)} %reduce-scatter.2.cloned.1.call-done), channel_id=1, replica_groups=mesh['dp'=4,'tensor'=8] {'dp'}, use_global_device_ids=true, to_apply=%region_29.31 | all-reduce | flops 14336 | bytes 114688 | tf_op jit(solution)/shard_map/psum | solution.py:88
  (220 shorter events, 177.8 us)
Async XLA Ops:
  7.2 180.1 %all-gather.5.cloned.1.call-start = ((), (), s32[]{:S(2)}) async-start(), calls=%async_computation.2 | async-start | bytes 5898240 | tf_op jit(solution)/shard_map/all_gather | solution.py:49
  7.9 1.2 copy-start.3
  7.9 428.9 %all-gather.3.cloned.1.call-start = ((), (), s32[]{:S(2)}) async-start(), calls=%async_computation.1 | async-start | bytes 52428800 | tf_op jit(solution)/shard_map/all_gather | solution.py:51
  8.7 1.0 copy-start.4
  8.7 936.9 %reduce-scatter.2.cloned.1.call-start = ((), (), s32[]{:S(2)}) async-start(), calls=%async_computation.3 | async-start | bytes 589824 | tf_op jit(solution)/shard_map/reduce_scatter | solution.py:87
  9.9 1.9 copy-start.17
  158.3 6.8 copy-start.20
  158.4 3.3 copy-start.18
  158.5 0.6 copy-start.13
  161.4 0.6 copy-start.5
  161.4 0.6 copy-start.7
  164.7 0.6 copy-start.9
  164.7 0.6 copy-start.11
  185.6 1.7 copy-start.1
  185.6 1.7 copy-start.22
  185.6 251.2 %copy-start.2 = (s32[256,2048]{0,1:T(8,128)S(1)}, s32[256,2048]{0,1:T(8,128)}, u32[]{:S(2)}) copy-start(s32[256,2048]{0,1:T(8,128)} %copy.11) | copy-start | bytes 6291460
  457.3 92.4 %collective-permute-start = (f32[256,2048]{0,1:T(8,128)}, f32[256,2048]{0,1:T(8,128)}, u32[]{:S(2)}, u32[]{:S(2)}) collective-permute-start(f32[256,2048]{0,1:T(8,128)} %fusion.3), channel_id=1, source_target_pairs={{0,4},{1,5},{2,6},{3,7},{4,0},{5,1},{6,2},{7,3},{8,12},{9,13},{10,... | collective-permute-start | bytes 6291464 | tf_op jit(solution)/shard_map/ppermute | solution.py:10
  462.7 23.7 %collective-permute-start.3 = (bf16[256,2048]{0,1:T(8,128)(2,1)}, bf16[256,2048]{0,1:T(8,128)(2,1)S(1)}, u32[]{:S(2)}, u32[]{:S(2)}) collective-permute-start(bf16[256,2048]{0,1:T(8,128)(2,1)} %get-tuple-element.11), channel_id=1, source_target_pairs={{0,1},{1,0},{2,3},{3,2},{4,5},{5,4},{6,7},{7,6},{8,9},{9,8},{10,11... | collective-permute-start | bytes 3145736 | tf_op jit(solution)/shard_map/ppermute | solution.py:10
  488.0 78.7 %collective-permute-start.4 = (bf16[256,2048]{0,1:T(8,128)(2,1)}, bf16[256,2048]{0,1:T(8,128)(2,1)}, u32[]{:S(2)}, u32[]{:S(2)}) collective-permute-start(bf16[256,2048]{0,1:T(8,128)(2,1)} %fusion.182), channel_id=1, source_target_pairs={{0,2},{1,3},{2,0},{3,1},{4,6},{5,7},{6,4},{7,5},{8,10},{9,11},{10,... | collective-permute-start | bytes 3145736 | tf_op jit(solution)/shard_map/ppermute | solution.py:10
  553.2 71.9 %collective-permute-start.1 = (f32[256,2048]{0,1:T(8,128)}, f32[256,2048]{0,1:T(8,128)}, u32[]{:S(2)}, u32[]{:S(2)}) collective-permute-start(f32[256,2048]{0,1:T(8,128)} %multiply_subtract_fusion.12), channel_id=1, source_target_pairs={{0,2},{1,3},{2,0},{3,1},{4,6},{5,7},{6,4},{7,5},{8,10},{9,11},{10,... | collective-permute-start | bytes 6291464 | tf_op jit(solution)/shard_map/ppermute | solution.py:10
  569.8 55.3 %collective-permute-start.5 = (bf16[256,2048]{0,1:T(8,128)(2,1)S(1)}, bf16[256,2048]{0,1:T(8,128)(2,1)S(1)}, u32[]{:S(2)}, u32[]{:S(2)}) collective-permute-start(bf16[256,2048]{0,1:T(8,128)(2,1)S(1)} %fusion.57), channel_id=1, source_target_pairs={{0,4},{1,5},{2,6},{3,7},{4,0},{5,1},{6,2},{7,3},{8,12},{9,13},{10,... | collective-permute-start | bytes 3145736 | tf_op jit(solution)/shard_map/ppermute | solution.py:10
  633.3 49.2 %collective-permute-start.2 = (f32[256,2048]{0,1:T(8,128)}, f32[256,2048]{0,1:T(8,128)}, u32[]{:S(2)}, u32[]{:S(2)}) collective-permute-start(f32[256,2048]{0,1:T(8,128)} %get-tuple-element.10), channel_id=1, source_target_pairs={{0,1},{1,0},{2,3},{3,2},{4,5},{5,4},{6,7},{7,6},{8,9},{9,8},{10,11... | collective-permute-start | bytes 6291464 | tf_op jit(solution)/shard_map/ppermute | solution.py:10
  728.6 0.7 copy-start.10
  728.7 0.7 copy-start.12
  728.7 0.7 copy-start.21
  735.0 0.7 copy-start.6
  735.0 0.7 copy-start.8
  735.0 0.7 copy-start.19
  743.6 151.2 %copy-start.24 = (pred[2048]{0:T(1024)(128)(4,1)S(1)}, pred[2048]{0:T(1024)(128)(4,1)}, u32[]{:S(2)}) copy-start(pred[2048]{0:T(1024)(128)(4,1)} %copy-done.23) | copy-start | bytes 6148
  918.2 2.9 copy-start
  918.2 2.9 copy-start.14
  918.2 2.8 copy-start.16
  (2 other events, 1.2 us)
Sparse Core Ops, SparseCore 0:
  9.6 57.1 all-gather.4
  68.7 368.0 all-gather.2
  918.3 27.1 reduce-scatter.1
where the time goes:
time: 986 us; the launch traced here: 971 us
  waiting for transfers between devices  386 us (39%)
  other arithmetic  315 us (32%)
  local copies, waits for them, and re-layouts  193 us (20%)
  blocking collectives  34.4 us (3%)
  matrix products  20.6 us (2%)
  between operations  15.6 us (2%)
    all_gather x1, waiting for transfers between devices, body(): lax.all_gather(codes, 'dp', axis=1, tiled=True).astype(jnp.float32)  249 us
    scatter-add x14, other arithmetic, scatter_terms(): return jnp.zeros((half_pairs,), jnp.float32).at[pair].add(term)  208 us
    gather x14, local copies, waits for them, and re-layouts, section_terms(): theta = jnp.take(table[section], pair)  165 us
    ppermute x6, waiting for transfers between devices, partner(): return lax.ppermute(value, axis, pairs)  115 us
    reduce_sum x12, other arithmetic, body(): jnp.sum(sign * grad * other, axis=0)  49 us
    add x10, other arithmetic, body(): field = cosine * field + signed * other  22.2 us
    reduce_scatter x1, waiting for transfers between devices, body(): lax.psum_scatter(collected, 'tensor', scatter_dimension=1, tiled=True)  20.9 us
    dot_general x1, matrix products, body(): lax.dot_general(full_cot, weight_piece, (((1,), (1,)), ((), ())), preferr...  20.6 us
  transfers between devices with their start and end apart: 9, of which 4 were waited for; matrix products, arithmetic and copies ran while one was open for 27% of the time, Pallas kernels for 0%

commit v1 on v0

v1 whole, which is shorter than its diff:
```python
import functools

import jax
import jax.numpy as jnp
from jax import lax
from jax.experimental import pallas as pl
from jax.experimental.pallas import tpu as pltpu
from jax.sharding import PartitionSpec as P

LANES = 128
LANE_BITS = 7
HIGH = lax.Precision.HIGHEST


def swap(value, axis, mask):
    pairs = [(source, source ^ mask) for source in range(lax.axis_size(axis))]
    return lax.ppermute(value, axis, pairs)


def pick(stacked, index):
    return lax.dynamic_index_in_dim(stacked, index, 0, keepdims=False)


def drop_bit(index, bit):
    return ((index >> (bit + 1)) << bit) | (index & ((1 << bit) - 1))


def lane_selectors(sections):
    lane = jnp.arange(LANES, dtype=jnp.int32)
    rows = []
    signs = []
    for section in range(sections):
        pair = drop_bit(lane, section)
        hot = pair[None, :] == jnp.arange(LANES // 2, dtype=jnp.int32)[:, None]
        rows.append(hot.astype(jnp.float32))
        signs.append(jnp.where((lane >> section) & 1 == 0, -1.0, 1.0).astype(jnp.float32))
    return jnp.stack(rows), jnp.stack(signs)


def local_tables(cosine, sine, width):
    local = cosine.shape[0]
    tiles = width // LANES
    hot, signs = lane_selectors(LANE_BITS)

    def lanes(values):
        shaped = values[:LANE_BITS].reshape(LANE_BITS, tiles, LANES // 2)
        return jnp.einsum("stk,skl->stl", shaped, hot, precision=HIGH)

    def whole(section, values, sign):
        step = 1 << (section - LANE_BITS)
        shaped = values.reshape(tiles // (2 * step), 1, step, LANES)
        return jnp.concatenate([sign * shaped, shaped], axis=1).reshape(1, tiles, LANES)

    cos_rows = [lanes(cosine)]
    sin_rows = [lanes(sine) * signs[:, None, :]]
    for section in range(LANE_BITS, local):
        cos_rows.append(whole(section, cosine[section], 1.0))
        sin_rows.append(whole(section, sine[section], -1.0))
    cos_table = jnp.concatenate(cos_rows, axis=0).reshape(local, width)
    sin_table = jnp.concatenate(sin_rows, axis=0).reshape(local, width)
    return cos_table, sin_table


def lane_partner(value, section):
    half = 1 << section
    lane = lax.broadcasted_iota(jnp.int32, value.shape, 1)
    up = pltpu.roll(value, half, 1)
    if 2 * half == LANES:
        return up
    down = pltpu.roll(value, LANES - half, 1)
    return jnp.where((lane & half) == 0, down, up)


def tile_at(tile):
    return pl.ds(tile * LANES, LANES)


def forward_kernel(local, act_ref, cos_ref, sin_ref, states_ref, last_ref):
    rows, width = act_ref.shape
    tiles = width // LANES
    step = 16

    def block(index, carry):
        at = pl.ds(pl.multiple_of(index * step, step), step)
        field = []
        for tile in range(tiles):
            value = act_ref[at, tile_at(tile)].astype(jnp.float32)
            for section in range(LANE_BITS):
                other = lane_partner(value, section)
                cosine = cos_ref[section : section + 1, tile_at(tile)]
                signed = sin_ref[section : section + 1, tile_at(tile)]
                value = cosine * value + signed * other
                states_ref[section, at, tile_at(tile)] = value
            field.append(value)
        for section in range(LANE_BITS, local):
            gap = 1 << (section - LANE_BITS)
            for tile in range(tiles):
                if tile & gap:
                    continue
                cosine = cos_ref[section : section + 1, tile_at(tile)]
                signed = sin_ref[section : section + 1, tile_at(tile)]
                low, high = field[tile], field[tile + gap]
                field[tile] = cosine * low + signed * high
                field[tile + gap] = cosine * high - signed * low
            for tile in range(tiles):
                states_ref[section, at, tile_at(tile)] = field[tile]
        for tile in range(tiles):
            last_ref[at, tile_at(tile)] = field[tile].astype(last_ref.dtype)
        return carry

    lax.fori_loop(0, rows // step, block, 0)


def forward_local(acts, cos_table, sin_table):
    rows, width = acts.shape
    local = cos_table.shape[0]
    block = min(rows, 32)
    table = pl.BlockSpec((local, width), lambda i: (0, 0))
    return pl.pallas_call(
        functools.partial(forward_kernel, local),
        grid=(rows // block,),
        in_specs=[pl.BlockSpec((block, width), lambda i: (i, 0)), table, table],
        out_specs=[
            pl.BlockSpec((local, block, width), lambda i: (0, i, 0)),
            pl.BlockSpec((block, width), lambda i: (i, 0)),
        ],
        out_shape=[
            jax.ShapeDtypeStruct((local, rows, width), jnp.float32),
            jax.ShapeDtypeStruct((rows, width), jnp.bfloat16),
        ],
        cost_estimate=pl.CostEstimate(
            flops=6 * local * rows * width,
            bytes_accessed=4 * (local + 1) * rows * width,
            transcendentals=0,
        ),
        name="forward_local",
    )(acts, cos_table, sin_table)


def backward_kernel(
    local, me_ref, grad_ref, states_ref, cos_ref, sin_ref, hot_ref,
    out_ref, lane_out, tile_out, lane_sum, tile_sum,
):
    rows, width = out_ref.shape
    tiles = width // LANES
    step = 16
    index = pl.program_id(0)

    @pl.when(index == 0)
    def _():
        lane_sum[...] = jnp.zeros_like(lane_sum)
        tile_sum[...] = jnp.zeros_like(tile_sum)

    def folded(value):
        return jnp.sum(value.reshape(step // 8, 8, LANES), axis=0)

    def block(number, carry):
        at = pl.ds(pl.multiple_of(number * step, step), step)
        grad = [grad_ref[0, at, tile_at(tile)] for tile in range(tiles)]
        for section in reversed(range(LANE_BITS, local)):
            gap = 1 << (section - LANE_BITS)
            for tile in range(tiles):
                if tile & gap:
                    continue
                cosine = cos_ref[section : section + 1, tile_at(tile)]
                signed = sin_ref[section : section + 1, tile_at(tile)]
                low, high = grad[tile], grad[tile + gap]
                before_low = states_ref[section, at, tile_at(tile)]
                before_high = states_ref[section, at, tile_at(tile + gap)]
                term = folded(high * before_low - low * before_high)
                place = drop_bit(tile, section - LANE_BITS)
                tile_sum[section - LANE_BITS, place] += term
                grad[tile] = cosine * low - signed * high
                grad[tile + gap] = cosine * high + signed * low
        for tile in range(tiles):
            value = grad[tile]
            for section in reversed(range(LANE_BITS)):
                cosine = cos_ref[section : section + 1, tile_at(tile)]
                signed = sin_ref[section : section + 1, tile_at(tile)]
                other = lane_partner(value, section)
                state = states_ref[section, at, tile_at(tile)]
                lane_sum[section, tile] += folded(other * state)
                value = cosine * value - signed * other
            out_ref[at, tile_at(tile)] = value.astype(out_ref.dtype)
        return carry

    lax.fori_loop(0, rows // step, block, 0)

    @pl.when(index == pl.num_programs(0) - 1)
    def _():
        for section in range(LANE_BITS):
            summed = jnp.sum(lane_sum[section], axis=1)
            lane_out[section] = lax.dot_general(
                summed,
                hot_ref[section],
                (((1,), (1,)), ((), ())),
                precision=HIGH,
                preferred_element_type=jnp.float32,
            )
        for section in range(local - LANE_BITS):
            tile_out[section] = jnp.sum(tile_sum[section], axis=1)


def backward_local(me, grads, states, cos_table, sin_table):
    pieces, rows, width = grads.shape
    local = cos_table.shape[0]
    tiles = width // LANES
    high = local - LANE_BITS
    hot, signs = lane_selectors(LANE_BITS)
    hot = -hot * signs[:, None, :]
    table = pl.BlockSpec((local, width), lambda i, m: (0, 0))
    return pl.pallas_call(
        functools.partial(backward_kernel, local),
        grid_spec=pltpu.PrefetchScalarGridSpec(
            num_scalar_prefetch=1,
            grid=(pieces,),
            in_specs=[
                pl.BlockSpec((1, rows, width), lambda i, m: (i, 0, 0)),
                pl.BlockSpec((local, rows, width), lambda i, m: (0, m[0] ^ i, 0)),
                table,
                table,
                pl.BlockSpec(hot.shape, lambda i, m: (0, 0, 0)),
            ],
            out_specs=[
                pl.BlockSpec((rows, width), lambda i, m: (m[0] ^ i, 0)),
                pl.BlockSpec((LANE_BITS, tiles, LANES // 2), lambda i, m: (0, 0, 0)),
                pl.BlockSpec((high, tiles // 2, LANES), lambda i, m: (0, 0, 0)),
            ],
            scratch_shapes=[
                pltpu.VMEM((LANE_BITS, tiles, 8, LANES), jnp.float32),
                pltpu.VMEM((high, tiles // 2, 8, LANES), jnp.float32),
            ],
        ),
        out_shape=[
            jax.ShapeDtypeStruct((pieces * rows, width), jnp.bfloat16),
            jax.ShapeDtypeStruct((LANE_BITS, tiles, LANES // 2), jnp.float32),
            jax.ShapeDtypeStruct((high, tiles // 2, LANES), jnp.float32),
        ],
        cost_estimate=pl.CostEstimate(
            flops=8 * local * pieces * rows * width,
            bytes_accessed=4 * (local + 2) * pieces * rows * width,
            transcendentals=0,
        ),
        name="backward_local",
    )(me, grads, states, cos_table, sin_table, hot)


def cross_kernel(count, bits, *refs):
    grad_refs = refs[:count]
    field_refs = refs[count : 2 * count]
    cos_ref, sin_ref = refs[2 * count : 2 * count + 2]
    out_refs = refs[2 * count + 2 : 3 * count + 2]
    term_ref = refs[3 * count + 2]
    rows, width = out_refs[0].shape
    step = 8
    for tile in range(width // LANES):
        at = tile_at(tile)
        totals = [[None] * (count // 2) for _ in range(bits)]
        for number in range(rows // step):
            part = pl.ds(number * step, step)
            field = [ref[part, at].astype(jnp.float32) for ref in field_refs]
            levels = [field]
            for bit in range(bits - 1):
                field = list(levels[-1])
                for low in range(count):
                    if low & (1 << bit):
                        continue
                    high = low | (1 << bit)
                    pair = drop_bit(low, bit)
                    cosine = cos_ref[bit, pair : pair + 1, at]
                    sine = sin_ref[bit, pair : pair + 1, at]
                    v_low, v_high = field[low], field[high]
                    field[low] = cosine * v_low - sine * v_high
                    field[high] = sine * v_low + cosine * v_high
                levels.append(field)
            grad = [ref[part, at].astype(jnp.float32) for ref in grad_refs]
            for bit in reversed(range(bits)):
                before = levels[bit]
                for low in range(count):
                    if low & (1 << bit):
                        continue
                    high = low | (1 << bit)
                    pair = drop_bit(low, bit)
                    cosine = cos_ref[bit, pair : pair + 1, at]
                    sine = sin_ref[bit, pair : pair + 1, at]
                    g_low, g_high = grad[low], grad[high]
                    grad[low] = cosine * g_low + sine * g_high
                    grad[high] = cosine * g_high - sine * g_low
                    term = grad[high] * before[low] - grad[low] * before[high]
                    held = totals[bit][pair]
                    totals[bit][pair] = term if held is None else held + term
            for ref, value in zip(out_refs, grad):
                ref[part, at] = value.astype(ref.dtype)
        for bit in range(bits):
            for pair in range(count // 2):
                term_ref[bit, pair : pair + 1, at] = jnp.sum(
                    totals[bit][pair], axis=0, keepdims=True
                )


def cross_sections(grads, fields, cos_table, sin_table):
    count = len(grads)
    bits = cos_table.shape[0]
    rows, width = grads[0].shape
    block = min(width, 256)
    piece = pl.BlockSpec((rows, block), lambda i: (0, i))
    table = pl.BlockSpec((bits, count // 2, block), lambda i: (0, 0, i))
    outs = pl.pallas_call(
        functools.partial(cross_kernel, count, bits),
        grid=(width // block,),
        in_specs=[piece] * (2 * count) + [table] * 2,
        out_specs=[piece] * count + [table],
        out_shape=[jax.ShapeDtypeStruct((rows, width), jnp.float32)] * count
        + [jax.ShapeDtypeStruct(cos_table.shape, jnp.float32)],
        cost_estimate=pl.CostEstimate(
            flops=12 * bits * count * rows * width,
            bytes_accessed=12 * count * rows * width,
            transcendentals=0,
        ),
        name="cross_sections",
    )(*grads, *fields, cos_table, sin_table)
    return outs[:count], outs[count]


def unpack_mask(words, rows, width):
    shifts = jnp.arange(16, dtype=jnp.int32)
    bits = jnp.bitwise_and(jnp.right_shift(words[:, None, :], shifts[None, :, None]), 1)
    return bits.reshape(rows, width).astype(jnp.float32)


def exchange(pieces, axis):
    return [pieces[0]] + [swap(pieces[m], axis, m) for m in range(1, len(pieces))]


def tree_sum(parts):
    while len(parts) > 1:
        parts = [parts[k] + parts[k + 1] for k in range(0, len(parts), 2)]
    return parts[0]


def body(activations, angles, clip_bits, codes, exponents, cotangent):
    rows, width = activations.shape
    sections, share = angles.shape
    groups = lax.axis_size("dp")
    count = lax.axis_size("tensor")
    ways = count // groups
    columns = codes.shape[1]
    part = columns // ways
    local = width.bit_length() - 1
    cross = sections - local
    me = lax.axis_index("tensor")
    mine = lax.axis_index("dp")
    level = me // ways
    core = me % ways

    blocks = jnp.stack(
        [cotangent] + [swap(cotangent, "tensor", m * ways) for m in range(1, groups)]
    )
    chosen = [pick(blocks, level ^ mine ^ m) for m in range(groups)]
    arrived = [chosen[0]] + [swap(chosen[m], "dp", m) for m in range(1, groups)]
    full = [
        jnp.concatenate([x] + [swap(x, "tensor", m) for m in range(1, ways)], axis=1)
        for x in arrived
    ]

    scale = jnp.exp2(exponents.astype(jnp.float32))
    weights = []
    for m in range(ways):
        at = (core ^ m) * part
        piece = lax.dynamic_slice_in_dim(codes, at, part, 1).astype(jnp.float32)
        factor = lax.dynamic_slice_in_dim(scale, mine * columns + at, part, 0)
        weights.append((piece * factor[None, :]).astype(jnp.bfloat16))
    weight = lax.optimization_barrier(jnp.concatenate(weights, axis=1))

    cosine = jnp.cos(angles)
    sine = jnp.sin(angles)
    cos_table, sin_table = local_tables(cosine[:local], sine[:local], width)
    states, last = forward_local(activations, cos_table, sin_table)

    order = me ^ jnp.arange(count, dtype=jnp.int32)
    trig = jnp.stack([cosine[local:], sine[local:]])
    around = jnp.stack([trig] + [swap(trig, "tensor", m) for m in range(1, count)])
    around = jnp.take(around, order, axis=0)
    around = jnp.moveaxis(around, 0, 2).reshape(2, cross, count // 2, width)
    jj = jnp.arange(count // 2, dtype=jnp.int32)
    cross_cos, cross_sin, flips = [], [], []
    for bit in range(cross):
        pair = drop_bit(me, bit) ^ jj
        flip = (1 - 2 * ((me >> bit) & 1)).astype(jnp.float32)
        flips.append(flip)
        cross_cos.append(jnp.take(around[0, bit], pair, axis=0))
        cross_sin.append(jnp.take(around[1, bit], pair, axis=0) * flip)
    cross_cos = jnp.stack(cross_cos)
    cross_sin = jnp.stack(cross_sin)

    last = last.reshape(count, rows // count, width)
    fields = exchange([pick(last, me ^ m) for m in range(count)], "tensor")

    products = [
        lax.dot_general(
            x, weight, (((1,), (1,)), ((), ())), preferred_element_type=jnp.float32
        )
        for x in full
    ]
    sent = [swap(products[m].astype(jnp.bfloat16), "dp", m) for m in range(1, groups)]
    total = products[0]
    for x in sent:
        total = total + x.astype(jnp.float32)
    grad = total * unpack_mask(clip_bits, rows, width)

    grad = grad.reshape(count, rows // count, width)
    grads = exchange([pick(grad, me ^ m) for m in range(count)], "tensor")
    grads, cross_terms = cross_sections(grads, fields, cross_cos, cross_sin)
    grads = jnp.stack(exchange(list(grads), "tensor"))

    natural = []
    for bit in range(cross):
        pair = drop_bit(me, bit) ^ jj
        natural.append(jnp.take(cross_terms[bit], pair, axis=0) * flips[bit])
    natural = jnp.stack(natural).reshape(cross, count, share)
    natural = jnp.moveaxis(natural, 1, 0)
    owned = tree_sum(exchange([pick(natural, me ^ m) for m in range(count)], "tensor"))

    input_grad, lane_terms, tile_terms = backward_local(
        me.reshape(1), grads, states, cos_table, sin_table
    )
    terms = jnp.concatenate(
        [
            lane_terms.reshape(LANE_BITS, share),
            tile_terms.reshape(local - LANE_BITS, share),
            owned,
        ],
        axis=0,
    )
    angle_grad = tree_sum([terms] + [swap(terms, "dp", m) for m in range(1, groups)])
    return (input_grad, angle_grad)


def solution(mesh):
    placed = (
        P("dp", "tensor"),
        P(None, "tensor"),
        P("dp", "tensor"),
        P("tensor", "dp"),
        P(),
        P("dp", "tensor"),
    )
    return jax.shard_map(
        body,
        mesh=mesh,
        in_specs=placed,
        out_specs=(P("dp", "tensor"), P(None, "tensor")),
        check_vma=False,
    )
```

time: 986 us -> 333 us (0.34); the launches traced: 971 us -> 332 us
  other arithmetic: 315 us -> 28.9 us
  waiting for transfers between devices: 386 us -> 171 us
  local copies, waits for them, and re-layouts: 193 us -> 19.8 us
  starting transfers between devices: 6.57 us -> 48.3 us
  Pallas kernels: 0 us -> 35.1 us
  blocking collectives: 34.4 us -> 0 us
  between operations: 15.6 us -> 1.63 us
    all_gather x2 -> x0, waiting for transfers between devices: 249 us -> none  [the longest x1 249 us: body(): lax.all_gather(codes, 'dp', axis=1, tiled=True).astype(jnp.float32)]
    scatter-add x14 -> x0, other arithmetic: 208 us -> none  [scatter_terms(): return jnp.zeros((half_pairs,), jnp.float32).at[pair].add(term)]
    gather x14 -> x10, local copies, waits for them, and re-layouts: 165 us -> 5.84 us  [the longest x3 1.71 us: body(): cross_sin.append(jnp.take(around[1, bit], pair, axis=0) * flip)]
    ppermute x6 -> x51, waiting for transfers between devices: 115 us -> 171 us  [swap(): return lax.ppermute(value, axis, pairs)]
    reduce_sum x12 -> x0, other arithmetic: 49 us -> none  [body(): jnp.sum(sign * grad * other, axis=0)]
    ppermute x6 -> x51, starting transfers between devices: 6.46 us -> 48.3 us  [swap(): return lax.ppermute(value, axis, pairs)]
    pallas_call x0 -> x3, Pallas kernels: none -> 35.1 us  [the longest x1 15.7 us: backward_local(): pl.pallas_call(functools.partial(backward_kernel, local), grid_spec=pltpu...]
    add x10 -> x2, other arithmetic: 22.2 us -> 0.67 us  [tree_sum(): parts = [parts[k] + parts[k + 1] for k in range(0, len(parts), 2)]]
  transfers between devices with their start and end apart: 9 -> 51, of which waited for: 4 -> 21; matrix products, arithmetic and copies ran while one was open for 27% -> 20% of each run, Pallas kernels for 0% -> 4%
where the time goes in v1:
time: 333 us; the launch traced here: 332 us
  waiting for transfers between devices  171 us (51%)
  starting transfers between devices  48.3 us (15%)
  Pallas kernels  35.1 us (11%)
  other arithmetic  28.9 us (9%)
  matrix products  26.7 us (8%)
  local copies, waits for them, and re-layouts  19.8 us (6%)
    ppermute x51, waiting for transfers between devices, swap(): return lax.ppermute(value, axis, pairs)  171 us
    ppermute x51, starting transfers between devices, swap(): return lax.ppermute(value, axis, pairs)  48.3 us
    dot_general x4, matrix products, body(): lax.dot_general(x, weight, (((1,), (1,)), ((), ())), preferred_element_ty...  26.3 us
    pallas_call x1, Pallas kernels, backward_local(): pl.pallas_call(functools.partial(backward_kernel, local), grid_spec=pltpu...  15.7 us
    pallas_call x1, Pallas kernels, forward_local(): pl.pallas_call(functools.partial(forward_kernel, local), grid=(rows // bl...  13.3 us
    convert_element_type x1, other arithmetic, body(): weights.append((piece * factor[None, :]).astype(jnp.bfloat16))  10 us
    concatenate x1, other arithmetic, body(): weight = lax.optimization_barrier(jnp.concatenate(weights, axis=1))  9.59 us
  transfers between devices with their start and end apart: 51, of which 21 were waited for; matrix products, arithmetic and copies ran while one was open for 20% of the time, Pallas kernels for 4%

profile of v1, /device:TPU:8, one launch (start us, length us, event | category | flops | bytes accessed | tf_op | source)
XLA Modules:
  0.0 331.7 jit_solution(4066926022078361307)
XLA Ops:
  4.4 2.6 collective-permute-start.1
  9.8 10.0 %multiply_convert_fusion.1 = (bf16[2048,1280]{1,0:T(8,128)(2,1)}, bf16[2048,1280]{1,0:T(8,128)(2,1)}) fusion(f32[1280]{0:T(1024)S(1)} %get-tuple-element.80, bf16[2048,2560]{1,0:T(8,128)(2,1)} %param.11, s32[]{:T(128)S(6)} %select_n.191, f32[1280]{0:T(1024)S(1)} %get-tuple-element.81, s32[]{:T(128)S(6)} %select_n.193), kind=kLoop, calls=%fused_computation.12 | loop fusion | flops 15728640 | bytes 20981768 | tf_op jit(solution)/shard_map/convert_element_type | solution.py:372
  19.8 9.6 %pad_maximum_fusion = bf16[2048,2560]{1,0:T(8,128)(2,1)} fusion(bf16[2048,1280]{1,0:T(8,128)(2,1)} %get-tuple-element.32, bf16[2048,1280]{1,0:T(8,128)(2,1)} %get-tuple-element.31), kind=kLoop, calls=%fused_computation.10 | loop fusion | flops 20971520 | bytes 20971520 | tf_op jit(solution)/shard_map/concatenate | solution.py:373
  32.0 13.3 %forward_local.1 = (f32[11,256,2048]{2,1,0:T(8,128)}, bf16[256,2048]{1,0:T(8,128)(2,1)}) custom-call(bf16[256,2048]{1,0:T(8,128)(2,1)} %act_ref.1, f32[11,2048]{1,0:T(8,128)} %concatenate.85.cos_ref, f32[11,2048]{1,0:T(8,128)} %concatenate.95.sin_ref), custom_call_target="tpu_custom_call" | custom-call | flops 34603008 | bytes 25165824 | tf_op jit(solution)/shard_map/forward_local/pallas_call | solution.py:119
  45.3 2.4 dynamic-slice_bitcast_fusion.12
  56.3 11.0 %collective-permute-done.2 = bf16[256,1280]{1,0:T(8,128)(2,1)S(1)} collective-permute-done((bf16[256,1280]{1,0:T(8,128)(2,1)}, bf16[256,1280]{1,0:T(8,128)(2,1)S(1)}, u32[]{:S(2)}, u32[]{:S(2)}) %collective-permute-start.2) | collective-permute-done | bytes 655392 | tf_op jit(solution)/shard_map/ppermute | solution.py:17
  74.9 10.6 %collective-permute-done.4 = bf16[256,1280]{1,0:T(8,128)(2,1)} collective-permute-done((bf16[256,1280]{1,0:T(8,128)(2,1)S(1)}, bf16[256,1280]{1,0:T(8,128)(2,1)}, u32[]{:S(2)}, u32[]{:S(2)}) %collective-permute-start.4) | collective-permute-done | bytes 655392 | tf_op jit(solution)/shard_map/ppermute | solution.py:17
  85.4 2.9 collective-permute-start.5
  89.5 14.4 %collective-permute-done.7 = bf16[256,1280]{1,0:T(8,128)(2,1)} collective-permute-done((bf16[256,1280]{1,0:T(8,128)(2,1)}, bf16[256,1280]{1,0:T(8,128)(2,1)}, u32[]{:S(2)}, u32[]{:S(2)}) %collective-permute-start.7) | collective-permute-done | bytes 655392 | tf_op jit(solution)/shard_map/ppermute | solution.py:17
  104.4 8.3 %convolution_convert_fusion.2 = bf16[256,2048]{1,0:T(8,128)(2,1)} fusion(bf16[2048,2560]{1,0:T(8,128)(2,1)} %pad_maximum_fusion, bf16[256,1280]{1,0:T(8,128)(2,1)} %collective-permute-done.5, bf16[256,1280]{1,0:T(8,128)(2,1)} %collective-permute-done.4), kind=kOutput, calls=%fused_computation.20 | convolution fusion | flops 2687500288 | bytes 12845056 | tf_op jit(solution)/shard_map/dot_general | solution.py:400
  113.2 5.0 %convolution_convert_fusion.1 = bf16[256,2048]{1,0:T(8,128)(2,1)} fusion(bf16[2048,2560]{1,0:T(8,128)(2,1)S(1)} %bitcast.206, bf16[256,1280]{1,0:T(8,128)(2,1)S(1)} %collective-permute-done.8, bf16[256,1280]{1,0:T(8,128)(2,1)} %collective-permute-done.7), kind=kOutput, calls=%fused_computation.19 | convolution fusion | flops 2687500288 | bytes 12845056 | tf_op jit(solution)/shard_map/dot_general | solution.py:400
  119.7 5.0 %convolution_convert_fusion = bf16[256,2048]{1,0:T(8,128)(2,1)} fusion(bf16[2048,2560]{1,0:T(8,128)(2,1)S(1)} %bitcast.206, bf16[256,1280]{1,0:T(8,128)(2,1)S(1)} %collective-permute-done.11, bf16[256,1280]{1,0:T(8,128)(2,1)} %collective-permute-done.10), kind=kOutput, calls=%fused_computation.18 | convolution fusion | flops 2687500288 | bytes 12845056 | tf_op jit(solution)/shard_map/dot_general | solution.py:400
  130.6 8.5 %collective-permute-done.6 = bf16[256,2048]{1,0:T(8,128)(2,1)} collective-permute-done((bf16[256,2048]{1,0:T(8,128)(2,1)}, bf16[256,2048]{1,0:T(8,128)(2,1)}, u32[]{:S(2)}, u32[]{:S(2)}) %collective-permute-start.6) | collective-permute-done | bytes 1048608 | tf_op jit(solution)/shard_map/ppermute | solution.py:17
  139.0 26.8 %collective-permute-done.9 = bf16[256,2048]{1,0:T(8,128)(2,1)} collective-permute-done((bf16[256,2048]{1,0:T(8,128)(2,1)}, bf16[256,2048]{1,0:T(8,128)(2,1)}, u32[]{:S(2)}, u32[]{:S(2)}) %collective-permute-start.9) | collective-permute-done | bytes 1048608 | tf_op jit(solution)/shard_map/ppermute | solution.py:17
  166.9 8.1 %fusion.2 = f32[256,2048]{1,0:T(8,128)S(1)} fusion(f32[256,2048]{1,0:T(8,128)S(1)} %copy-done.1, bf16[2048,2560]{1,0:T(8,128)(2,1)} %pad_maximum_fusion, bf16[256,2048]{1,0:T(8,128)(2,1)} %collective-permute-done.12, bf16[256,2048]{1,0:T(8,128)(2,1)} %collective-permute-done.9, bf16[256,2048]{1,0:T(8,128)(2,1)} %collective-permute-done.6, ...), kind=kOutput, calls=%fused_computation.17 | convolution fusion | flops 2690646016 | bytes 19136512 | tf_op jit(solution)/shard_map/dot_general | solution.py:400
  176.7 2.9 collective-permute-start.26
  181.6 5.7 %collective-permute-done.25.refs_14_ = bf16[32,2048]{1,0:T(8,128)(2,1)S(1)} collective-permute-done((bf16[32,2048]{1,0:T(8,128)(2,1)S(1)}, bf16[32,2048]{1,0:T(8,128)(2,1)S(1)}, u32[]{:S(2)}, u32[]{:S(2)}) %collective-permute-start.25) | collective-permute-done | bytes 131104 | tf_op jit(solution)/shard_map/ppermute | solution.py:17
  187.4 4.1 %collective-permute-done.26.refs_15_ = bf16[32,2048]{1,0:T(8,128)(2,1)S(1)} collective-permute-done((bf16[32,2048]{1,0:T(8,128)(2,1)S(1)}, bf16[32,2048]{1,0:T(8,128)(2,1)S(1)}, u32[]{:S(2)}, u32[]{:S(2)}) %collective-permute-start.26) | collective-permute-done | bytes 131104 | tf_op jit(solution)/shard_map/ppermute | solution.py:17
  192.1 4.7 %collective-permute-done.14.refs_2_ = f32[32,2048]{1,0:T(8,128)S(1)} collective-permute-done((f32[32,2048]{1,0:T(8,128)S(1)}, f32[32,2048]{1,0:T(8,128)S(1)}, u32[]{:S(2)}, u32[]{:S(2)}) %collective-permute-start.14) | collective-permute-done | bytes 262176 | tf_op jit(solution)/shard_map/ppermute | solution.py:17
  199.7 2.7 collective-permute-done.15.refs_3_
  202.9 19.3 %collective-permute-done.17.refs_5_ = f32[32,2048]{1,0:T(8,128)S(1)} collective-permute-done((f32[32,2048]{1,0:T(8,128)S(1)}, f32[32,2048]{1,0:T(8,128)S(1)}, u32[]{:S(2)}, u32[]{:S(2)}) %collective-permute-start.17) | collective-permute-done | bytes 262176 | tf_op jit(solution)/shard_map/ppermute | solution.py:17
  222.2 7.3 %collective-permute-done.18.refs_6_ = f32[32,2048]{1,0:T(8,128)S(1)} collective-permute-done((f32[32,2048]{1,0:T(8,128)S(1)}, f32[32,2048]{1,0:T(8,128)S(1)}, u32[]{:S(2)}, u32[]{:S(2)}) %collective-permute-start.18) | collective-permute-done | bytes 262176 | tf_op jit(solution)/shard_map/ppermute | solution.py:17
  229.5 6.3 %collective-permute-done.19.refs_7_ = f32[32,2048]{1,0:T(8,128)S(1)} collective-permute-done((f32[32,2048]{1,0:T(8,128)S(1)}, f32[32,2048]{1,0:T(8,128)S(1)}, u32[]{:S(2)}, u32[]{:S(2)}) %collective-permute-start.19) | collective-permute-done | bytes 262176 | tf_op jit(solution)/shard_map/ppermute | solution.py:17
  236.5 6.2 %cross_sections.1 = (f32[32,2048]{1,0:T(8,128)}, f32[32,2048]{1,0:T(8,128)}, f32[32,2048]{1,0:T(8,128)}, f32[32,2048]{1,0:T(8,128)}, f32[32,2048]{1,0:T(8,128)},...) custom-call(f32[32,2048]{1,0:T(8,128)} %get-tuple-element.44.refs_0_, ...), custom_call_target="tpu_custom_call" | custom-call | flops 18874368 | bytes 6291456 | tf_op jit(solution)/shard_map/cross_sections/pallas_call | solution.py:308
  248.9 2.2 collective-permute-start.45
  259.4 11.4 %collective-permute-done.35 = f32[32,2048]{1,0:T(8,128)S(1)} collective-permute-done((f32[32,2048]{1,0:T(8,128)}, f32[32,2048]{1,0:T(8,128)S(1)}, u32[]{:S(2)}, u32[]{:S(2)}) %collective-permute-start.35) | collective-permute-done | bytes 262176 | tf_op jit(solution)/shard_map/ppermute | solution.py:17
  270.8 5.0 %collective-permute-done.36 = f32[32,2048]{1,0:T(8,128)S(1)} collective-permute-done((f32[32,2048]{1,0:T(8,128)}, f32[32,2048]{1,0:T(8,128)S(1)}, u32[]{:S(2)}, u32[]{:S(2)}) %collective-permute-start.36) | collective-permute-done | bytes 262176 | tf_op jit(solution)/shard_map/ppermute | solution.py:17
  275.9 16.3 %collective-permute-done.38 = f32[32,2048]{1,0:T(8,128)S(1)} collective-permute-done((f32[32,2048]{1,0:T(8,128)S(1)}, f32[32,2048]{1,0:T(8,128)S(1)}, u32[]{:S(2)}, u32[]{:S(2)}) %collective-permute-start.38) | collective-permute-done | bytes 262176 | tf_op jit(solution)/shard_map/ppermute | solution.py:17
  292.2 7.4 %collective-permute-done.39 = f32[32,2048]{1,0:T(8,128)S(1)} collective-permute-done((f32[32,2048]{1,0:T(8,128)S(1)}, f32[32,2048]{1,0:T(8,128)S(1)}, u32[]{:S(2)}, u32[]{:S(2)}) %collective-permute-start.39) | collective-permute-done | bytes 262176 | tf_op jit(solution)/shard_map/ppermute | solution.py:17
  299.7 4.4 %collective-permute-done.40 = f32[32,2048]{1,0:T(8,128)S(1)} collective-permute-done((f32[32,2048]{1,0:T(8,128)S(1)}, f32[32,2048]{1,0:T(8,128)S(1)}, u32[]{:S(2)}, u32[]{:S(2)}) %collective-permute-start.40) | collective-permute-done | bytes 262176 | tf_op jit(solution)/shard_map/ppermute | solution.py:17
  305.5 15.7 %backward_local.1 = (bf16[256,2048]{1,0:T(8,128)(2,1)}, f32[7,16,64]{2,1,0:T(8,128)}, f32[4,8,128]{2,1,0:T(8,128)}) custom-call(s32[1]{0:T(128)} %bitcast.me_ref, f32[8,32,2048]{2,1,0:T(8,128)} %copy-done, f32[11,256,2048]{2,1,0:T(8,128)} %get-tuple-element.26.states_ref, f32[11,2048]{1,0:T(8,128)} %concatenate.85.cos_ref, f32[11,2048]{1,0:T(8,128)} %concatenate.95.sin_ref, ...), custom_call_target="tpu_custom_call" | custom-call | flops 46137344 | bytes 27262976 | tf_op jit(solution)/shard_map/backward_local/pallas_call | solution.py:212
  328.6 2.4 collective-permute-done.50
  (273 shorter events, 67.7 us)
Async XLA Ops:
  2.4 48.0 %collective-permute-start.27 = (f32[2,3,1024]{2,1,0:T(4,128)}, f32[2,3,1024]{2,1,0:T(4,128)S(1)}, u32[]{:S(2)}, u32[]{:S(2)}) collective-permute-start(f32[2,3,1024]{2,1,0:T(4,128)} %pad_maximum_fusion.5), channel_id=1, source_target_pairs={{0,1},{1,0},{2,3},{3,2},{4,5},{5,4},{6,7},{7,6},{8,9},{9,8},{10,11... | collective-permute-start | bytes 73736 | tf_op jit(solution)/shard_map/ppermute | solution.py:17
  2.4 48.8 %collective-permute-start.28 = (f32[2,3,1024]{2,1,0:T(4,128)}, f32[2,3,1024]{2,1,0:T(4,128)S(1)}, u32[]{:S(2)}, u32[]{:S(2)}) collective-permute-start(f32[2,3,1024]{2,1,0:T(4,128)} %pad_maximum_fusion.5), channel_id=1, source_target_pairs={{0,2},{1,3},{2,0},{3,1},{4,6},{5,7},{6,4},{7,5},{8,10},{9,11},{10,... | collective-permute-start | bytes 73736 | tf_op jit(solution)/shard_map/ppermute | solution.py:17
  2.4 51.0 %collective-permute-start = (bf16[256,1280]{1,0:T(8,128)(2,1)}, bf16[256,1280]{1,0:T(8,128)(2,1)S(1)}, u32[]{:S(2)}, u32[]{:S(2)}) collective-permute-start(bf16[256,1280]{1,0:T(8,128)(2,1)} %param.13), channel_id=1, source_target_pairs={{0,2},{1,3},{2,0},{3,1},{4,6},{5,7},{6,4},{7,5},{8,10},{9,11},{10,... | collective-permute-start | bytes 1966088 | tf_op jit(solution)/shard_map/ppermute | solution.py:17
  4.4 50.4 %collective-permute-start.1 = (bf16[256,1280]{1,0:T(8,128)(2,1)}, bf16[256,1280]{1,0:T(8,128)(2,1)S(1)}, u32[]{:S(2)}, u32[]{:S(2)}) collective-permute-start(bf16[256,1280]{1,0:T(8,128)(2,1)} %param.13), channel_id=1, source_target_pairs={{0,4},{1,5},{2,6},{3,7},{4,0},{5,1},{6,2},{7,3},{8,12},{9,13},{10,... | collective-permute-start | bytes 1966088 | tf_op jit(solution)/shard_map/ppermute | solution.py:17
  7.0 60.4 %collective-permute-start.2 = (bf16[256,1280]{1,0:T(8,128)(2,1)}, bf16[256,1280]{1,0:T(8,128)(2,1)S(1)}, u32[]{:S(2)}, u32[]{:S(2)}) collective-permute-start(bf16[256,1280]{1,0:T(8,128)(2,1)} %param.13), channel_id=1, source_target_pairs={{0,6},{1,7},{2,4},{3,5},{4,2},{5,3},{6,0},{7,1},{8,14},{9,15},{10,... | collective-permute-start | bytes 1966088 | tf_op jit(solution)/shard_map/ppermute | solution.py:17
  50.4 18.7 %collective-permute-start.29 = (f32[2,3,1024]{2,1,0:T(4,128)}, f32[2,3,1024]{2,1,0:T(4,128)S(1)}, u32[]{:S(2)}, u32[]{:S(2)}) collective-permute-start(f32[2,3,1024]{2,1,0:T(4,128)} %pad_maximum_fusion.5), channel_id=1, source_target_pairs={{0,3},{1,2},{2,1},{3,0},{4,7},{5,6},{6,5},{7,4},{8,11},{9,10},{10,... | collective-permute-start | bytes 73736 | tf_op jit(solution)/shard_map/ppermute | solution.py:17
  51.2 19.4 %collective-permute-start.30 = (f32[2,3,1024]{2,1,0:T(4,128)}, f32[2,3,1024]{2,1,0:T(4,128)S(1)}, u32[]{:S(2)}, u32[]{:S(2)}) collective-permute-start(f32[2,3,1024]{2,1,0:T(4,128)} %pad_maximum_fusion.5), channel_id=1, source_target_pairs={{0,4},{1,5},{2,6},{3,7},{4,0},{5,1},{6,2},{7,3},{8,12},{9,13},{10,... | collective-permute-start | bytes 73736 | tf_op jit(solution)/shard_map/ppermute | solution.py:17
  53.3 19.4 %collective-permute-start.31 = (f32[2,3,1024]{2,1,0:T(4,128)}, f32[2,3,1024]{2,1,0:T(4,128)S(1)}, u32[]{:S(2)}, u32[]{:S(2)}) collective-permute-start(f32[2,3,1024]{2,1,0:T(4,128)} %pad_maximum_fusion.5), channel_id=1, source_target_pairs={{0,5},{1,4},{2,7},{3,6},{4,1},{5,0},{6,3},{7,2},{8,13},{9,12},{10,... | collective-permute-start | bytes 73736 | tf_op jit(solution)/shard_map/ppermute | solution.py:17
  54.7 19.6 %collective-permute-start.32 = (f32[2,3,1024]{2,1,0:T(4,128)}, f32[2,3,1024]{2,1,0:T(4,128)S(1)}, u32[]{:S(2)}, u32[]{:S(2)}) collective-permute-start(f32[2,3,1024]{2,1,0:T(4,128)} %pad_maximum_fusion.5), channel_id=1, source_target_pairs={{0,6},{1,7},{2,4},{3,5},{4,2},{5,3},{6,0},{7,1},{8,14},{9,15},{10,... | collective-permute-start | bytes 73736 | tf_op jit(solution)/shard_map/ppermute | solution.py:17
  67.3 21.0 %collective-permute-start.33 = (f32[2,3,1024]{2,1,0:T(4,128)}, f32[2,3,1024]{2,1,0:T(4,128)S(1)}, u32[]{:S(2)}, u32[]{:S(2)}) collective-permute-start(f32[2,3,1024]{2,1,0:T(4,128)} %pad_maximum_fusion.5), channel_id=1, source_target_pairs={{0,7},{1,6},{2,5},{3,4},{4,3},{5,2},{6,1},{7,0},{8,15},{9,14},{10,... | collective-permute-start | bytes 73736 | tf_op jit(solution)/shard_map/ppermute | solution.py:17
  69.1 16.3 %collective-permute-start.4 = (bf16[256,1280]{1,0:T(8,128)(2,1)S(1)}, bf16[256,1280]{1,0:T(8,128)(2,1)}, u32[]{:S(2)}, u32[]{:S(2)}) collective-permute-start(bf16[256,1280]{1,0:T(8,128)(2,1)S(1)} %get-tuple-element.36), channel_id=1, source_target_pairs={{0,8},{8,0},{16,24},{24,16},{1,9},{9,1},{17,25},{25,17},{2,10},{10... | collective-permute-start | bytes 1966088 | tf_op jit(solution)/shard_map/ppermute | solution.py:17
  70.6 105.4 %collective-permute-start.20 = (bf16[32,2048]{1,0:T(8,128)(2,1)}, bf16[32,2048]{1,0:T(8,128)(2,1)}, u32[]{:S(2)}, u32[]{:S(2)}) collective-permute-start(bf16[32,2048]{1,0:T(8,128)(2,1)} %get-tuple-element.51), channel_id=1, source_target_pairs={{0,1},{1,0},{2,3},{3,2},{4,5},{5,4},{6,7},{7,6},{8,9},{9,8},{10,11... | collective-permute-start | bytes 393224 | tf_op jit(solution)/shard_map/ppermute | solution.py:17
  72.8 31.1 %collective-permute-start.7 = (bf16[256,1280]{1,0:T(8,128)(2,1)}, bf16[256,1280]{1,0:T(8,128)(2,1)}, u32[]{:S(2)}, u32[]{:S(2)}) collective-permute-start(bf16[256,1280]{1,0:T(8,128)(2,1)} %get-tuple-element.35), channel_id=1, source_target_pairs={{0,16},{8,24},{16,0},{24,8},{1,17},{9,25},{17,1},{25,9},{2,18},{10... | collective-permute-start | bytes 1966088 | tf_op jit(solution)/shard_map/ppermute | solution.py:17
  74.4 29.5 %collective-permute-start.10 = (bf16[256,1280]{1,0:T(8,128)(2,1)}, bf16[256,1280]{1,0:T(8,128)(2,1)}, u32[]{:S(2)}, u32[]{:S(2)}) collective-permute-start(bf16[256,1280]{1,0:T(8,128)(2,1)} %get-tuple-element.34), channel_id=1, source_target_pairs={{0,24},{8,16},{16,8},{24,0},{1,25},{9,17},{17,9},{25,1},{2,26},{10... | collective-permute-start | bytes 1966088 | tf_op jit(solution)/shard_map/ppermute | solution.py:17
  85.4 19.0 %collective-permute-start.5 = (bf16[256,1280]{1,0:T(8,128)(2,1)}, bf16[256,1280]{1,0:T(8,128)(2,1)}, u32[]{:S(2)}, u32[]{:S(2)}) collective-permute-start(bf16[256,1280]{1,0:T(8,128)(2,1)} %collective-permute-done.4), channel_id=1, source_target_pairs={{0,1},{1,0},{2,3},{3,2},{4,5},{5,4},{6,7},{7,6},{8,9},{9,8},{10,11... | collective-permute-start | bytes 1966088 | tf_op jit(solution)/shard_map/ppermute | solution.py:17
  103.9 15.9 %collective-permute-start.11 = (bf16[256,1280]{1,0:T(8,128)(2,1)}, bf16[256,1280]{1,0:T(8,128)(2,1)S(1)}, u32[]{:S(2)}, u32[]{:S(2)}) collective-permute-start(bf16[256,1280]{1,0:T(8,128)(2,1)} %collective-permute-done.10), channel_id=1, source_target_pairs={{0,1},{1,0},{2,3},{3,2},{4,5},{5,4},{6,7},{7,6},{8,9},{9,8},{10,11... | collective-permute-start | bytes 1966088 | tf_op jit(solution)/shard_map/ppermute | solution.py:17
  112.7 26.3 %collective-permute-start.6 = (bf16[256,2048]{1,0:T(8,128)(2,1)}, bf16[256,2048]{1,0:T(8,128)(2,1)}, u32[]{:S(2)}, u32[]{:S(2)}) collective-permute-start(bf16[256,2048]{1,0:T(8,128)(2,1)} %convolution_convert_fusion.2), channel_id=1, source_target_pairs={{0,8},{8,0},{16,24},{24,16},{1,9},{9,1},{17,25},{25,17},{2,10},{10... | collective-permute-start | bytes 3145736 | tf_op jit(solution)/shard_map/ppermute | solution.py:17
  118.2 47.6 %collective-permute-start.9 = (bf16[256,2048]{1,0:T(8,128)(2,1)}, bf16[256,2048]{1,0:T(8,128)(2,1)}, u32[]{:S(2)}, u32[]{:S(2)}) collective-permute-start(bf16[256,2048]{1,0:T(8,128)(2,1)} %convolution_convert_fusion.1), channel_id=1, source_target_pairs={{0,16},{8,24},{16,0},{24,8},{1,17},{9,25},{17,1},{25,9},{2,18},{10... | collective-permute-start | bytes 3145736 | tf_op jit(solution)/shard_map/ppermute | solution.py:17
  124.7 41.1 %collective-permute-start.12 = (bf16[256,2048]{1,0:T(8,128)(2,1)}, bf16[256,2048]{1,0:T(8,128)(2,1)}, u32[]{:S(2)}, u32[]{:S(2)}) collective-permute-start(bf16[256,2048]{1,0:T(8,128)(2,1)} %convolution_convert_fusion), channel_id=1, source_target_pairs={{0,24},{8,16},{16,8},{24,0},{1,25},{9,17},{17,9},{25,1},{2,26},{10... | collective-permute-start | bytes 3145736 | tf_op jit(solution)/shard_map/ppermute | solution.py:17
  130.5 46.2 %collective-permute-start.21 = (bf16[32,2048]{1,0:T(8,128)(2,1)}, bf16[32,2048]{1,0:T(8,128)(2,1)S(1)}, u32[]{:S(2)}, u32[]{:S(2)}) collective-permute-start(bf16[32,2048]{1,0:T(8,128)(2,1)} %get-tuple-element.50), channel_id=1, source_target_pairs={{0,2},{1,3},{2,0},{3,1},{4,6},{5,7},{6,4},{7,5},{8,10},{9,11},{10,... | collective-permute-start | bytes 393224 | tf_op jit(solution)/shard_map/ppermute | solution.py:17
  139.0 40.6 %collective-permute-start.22 = (bf16[32,2048]{1,0:T(8,128)(2,1)}, bf16[32,2048]{1,0:T(8,128)(2,1)S(1)}, u32[]{:S(2)}, u32[]{:S(2)}) collective-permute-start(bf16[32,2048]{1,0:T(8,128)(2,1)} %get-tuple-element.49), channel_id=1, source_target_pairs={{0,3},{1,2},{2,1},{3,0},{4,7},{5,6},{6,5},{7,4},{8,11},{9,10},{10,... | collective-permute-start | bytes 393224 | tf_op jit(solution)/shard_map/ppermute | solution.py:17
  179.6 17.2 %collective-permute-start.14 = (f32[32,2048]{1,0:T(8,128)S(1)}, f32[32,2048]{1,0:T(8,128)S(1)}, u32[]{:S(2)}, u32[]{:S(2)}) collective-permute-start(f32[32,2048]{1,0:T(8,128)S(1)} %get-tuple-element.42), channel_id=1, source_target_pairs={{0,2},{1,3},{2,0},{3,1},{4,6},{5,7},{6,4},{7,5},{8,10},{9,11},{10,... | collective-permute-start | bytes 786440 | tf_op jit(solution)/shard_map/ppermute | solution.py:17
  181.4 21.0 %collective-permute-start.15 = (f32[32,2048]{1,0:T(8,128)S(1)}, f32[32,2048]{1,0:T(8,128)S(1)}, u32[]{:S(2)}, u32[]{:S(2)}) collective-permute-start(f32[32,2048]{1,0:T(8,128)S(1)} %get-tuple-element.41), channel_id=1, source_target_pairs={{0,3},{1,2},{2,1},{3,0},{4,7},{5,6},{6,5},{7,4},{8,11},{9,10},{10,... | collective-permute-start | bytes 786440 | tf_op jit(solution)/shard_map/ppermute | solution.py:17
  191.5 30.7 %collective-permute-start.17 = (f32[32,2048]{1,0:T(8,128)S(1)}, f32[32,2048]{1,0:T(8,128)S(1)}, u32[]{:S(2)}, u32[]{:S(2)}) collective-permute-start(f32[32,2048]{1,0:T(8,128)S(1)} %get-tuple-element.39), channel_id=1, source_target_pairs={{0,5},{1,4},{2,7},{3,6},{4,1},{5,0},{6,3},{7,2},{8,13},{9,12},{10,... | collective-permute-start | bytes 786440 | tf_op jit(solution)/shard_map/ppermute | solution.py:17
  191.5 38.0 %collective-permute-start.18 = (f32[32,2048]{1,0:T(8,128)S(1)}, f32[32,2048]{1,0:T(8,128)S(1)}, u32[]{:S(2)}, u32[]{:S(2)}) collective-permute-start(f32[32,2048]{1,0:T(8,128)S(1)} %get-tuple-element.38), channel_id=1, source_target_pairs={{0,6},{1,7},{2,4},{3,5},{4,2},{5,3},{6,0},{7,1},{8,14},{9,15},{10,... | collective-permute-start | bytes 786440 | tf_op jit(solution)/shard_map/ppermute | solution.py:17
  196.8 39.0 %collective-permute-start.19 = (f32[32,2048]{1,0:T(8,128)S(1)}, f32[32,2048]{1,0:T(8,128)S(1)}, u32[]{:S(2)}, u32[]{:S(2)}) collective-permute-start(f32[32,2048]{1,0:T(8,128)S(1)} %get-tuple-element.37), channel_id=1, source_target_pairs={{0,7},{1,6},{2,5},{3,4},{4,3},{5,2},{6,1},{7,0},{8,15},{9,14},{10,... | collective-permute-start | bytes 786440 | tf_op jit(solution)/shard_map/ppermute | solution.py:17
  253.3 17.5 %collective-permute-start.35 = (f32[32,2048]{1,0:T(8,128)}, f32[32,2048]{1,0:T(8,128)S(1)}, u32[]{:S(2)}, u32[]{:S(2)}) collective-permute-start(f32[32,2048]{1,0:T(8,128)} %get-tuple-element.20), channel_id=1, source_target_pairs={{0,2},{1,3},{2,0},{3,1},{4,6},{5,7},{6,4},{7,5},{8,10},{9,11},{10,... | collective-permute-start | bytes 786440 | tf_op jit(solution)/shard_map/ppermute | solution.py:17
  255.3 20.6 %collective-permute-start.36 = (f32[32,2048]{1,0:T(8,128)}, f32[32,2048]{1,0:T(8,128)S(1)}, u32[]{:S(2)}, u32[]{:S(2)}) collective-permute-start(f32[32,2048]{1,0:T(8,128)} %get-tuple-element.21), channel_id=1, source_target_pairs={{0,3},{1,2},{2,1},{3,0},{4,7},{5,6},{6,5},{7,4},{8,11},{9,10},{10,... | collective-permute-start | bytes 786440 | tf_op jit(solution)/shard_map/ppermute | solution.py:17
  255.4 20.5 %collective-permute-start.37 = (f32[32,2048]{1,0:T(8,128)}, f32[32,2048]{1,0:T(8,128)S(1)}, u32[]{:S(2)}, u32[]{:S(2)}) collective-permute-start(f32[32,2048]{1,0:T(8,128)} %get-tuple-element.22), channel_id=1, source_target_pairs={{0,4},{1,5},{2,6},{3,7},{4,0},{5,1},{6,2},{7,3},{8,12},{9,13},{10,... | collective-permute-start | bytes 786440 | tf_op jit(solution)/shard_map/ppermute | solution.py:17
  257.2 35.0 %collective-permute-start.38 = (f32[32,2048]{1,0:T(8,128)S(1)}, f32[32,2048]{1,0:T(8,128)S(1)}, u32[]{:S(2)}, u32[]{:S(2)}) collective-permute-start(f32[32,2048]{1,0:T(8,128)S(1)} %copy-done.30), channel_id=1, source_target_pairs={{0,5},{1,4},{2,7},{3,6},{4,1},{5,0},{6,3},{7,2},{8,13},{9,12},{10,... | collective-permute-start | bytes 786440 | tf_op jit(solution)/shard_map/ppermute | solution.py:17
  258.7 40.9 %collective-permute-start.39 = (f32[32,2048]{1,0:T(8,128)S(1)}, f32[32,2048]{1,0:T(8,128)S(1)}, u32[]{:S(2)}, u32[]{:S(2)}) collective-permute-start(f32[32,2048]{1,0:T(8,128)S(1)} %copy-done.29), channel_id=1, source_target_pairs={{0,6},{1,7},{2,4},{3,5},{4,2},{5,3},{6,0},{7,1},{8,14},{9,15},{10,... | collective-permute-start | bytes 786440 | tf_op jit(solution)/shard_map/ppermute | solution.py:17
  270.8 33.3 %collective-permute-start.40 = (f32[32,2048]{1,0:T(8,128)S(1)}, f32[32,2048]{1,0:T(8,128)S(1)}, u32[]{:S(2)}, u32[]{:S(2)}) collective-permute-start(f32[32,2048]{1,0:T(8,128)S(1)} %copy-done.28), channel_id=1, source_target_pairs={{0,7},{1,6},{2,5},{3,4},{4,3},{5,2},{6,1},{7,0},{8,15},{9,14},{10,... | collective-permute-start | bytes 786440 | tf_op jit(solution)/shard_map/ppermute | solution.py:17
  (53 other events, 1084.1 us)
